TPU v7x, 256 devices: a whole 4x4x8 slice. The times are simulated.
256 devices in a mesh: row: 16 (over y_hi, x, core), col: 16 (over y_lo, z).
Axes of the slice: x: 4, y: 4 (y_hi: 2, y_lo: 2; y = y_hi * 2 + y_lo), z: 8, core: 2. Of those that a mesh axis runs over, the one named last changes fastest.
Arguments:
- tokens: bfloat16 [8192, 6144], P('row', 'col'), may hold values from -6 to 6
- gate_weight: bfloat16 [6144, 12288], P('row', 'col'), may hold values from -0.078125 to 0.078125
- up_weight: bfloat16 [6144, 12288], P('row', 'col'), may hold values from -0.078125 to 0.078125
Outputs:
- hidden: float32 [8192, 12288], P('row', 'col')
All inputs are finite; a program needn't handle non-finite values.
Results may differ from a plain program's by a relative error of at most 0.0003.
Values may be sent and summed in bfloat16 or wider, within the bound.
No kernel may reach another device: no remote copies, remote signals or barrier semaphores. Data moves between devices by JAX's collectives and lax.ppermute only.
A program may use at most 128 MiB of HBM per device.

v0:
```python
import jax
import jax.numpy as jnp
from jax import lax
from jax.sharding import PartitionSpec as P


def accumulate(gathered, weight_rows):
    return jnp.dot(gathered, weight_rows, preferred_element_type=jnp.float32)


def per_device(tokens, gate_weight, up_weight):
    gathered = lax.all_gather(tokens, "col", axis=1, tiled=True)

    def add_single(weight_rows):
        return accumulate(gathered, weight_rows)

    gate_sum = add_single(lax.all_gather(gate_weight, "row", axis=0, tiled=True))
    up_sum = add_single(lax.all_gather(up_weight, "row", axis=0, tiled=True))
    return jax.nn.silu(gate_sum) * up_sum


def solution(mesh):
    in_specs = (P("row", "col"), P("row", "col"), P("row", "col"))
    out_specs = P("row", "col")
    return jax.shard_map(
        per_device, mesh=mesh, in_specs=in_specs, out_specs=out_specs, check_vma=False
    )
```

profile of v0, /device:TPU:1, one launch (start us, length us, event | category | flops | bytes accessed | tf_op | source)
XLA Modules:
  0.0 278.8 jit_solution(5414926896950332376)
XLA Ops:
  6.5 0.0 all-gather.4.cloned.1.call-start
  6.5 0.7 all-gather.4.cloned.1.call-update
  7.3 0.0 all-gather.6.cloned.1.call-start
  7.3 0.7 all-gather.6.cloned.1.call-update
  8.0 0.0 all-gather.8.cloned.1.call-start
  8.1 0.7 all-gather.8.cloned.1.call-update
  8.7 82.3 %all-gather.4.cloned.1.call-done = bf16[512,6144]{1,0:T(8,128)(2,1)} async-done(((bf16[512,384]{1,0:T(8,128)(2,1)}), bf16[512,6144]{1,0:T(8,128)(2,1)}) %all-gather.4.cloned.1.call-update) | async-done | bytes 6291472 | tf_op jit(solution)/shard_map/all_gather | solution.py:12
  91.1 87.6 %all-gather.6.cloned.1.call-done = bf16[6144,768]{1,0:T(8,128)(2,1)} async-done(((bf16[384,768]{1,0:T(8,128)(2,1)}), bf16[6144,768]{1,0:T(8,128)(2,1)}) %all-gather.6.cloned.1.call-update) | async-done | bytes 9437200 | tf_op jit(solution)/shard_map/all_gather | solution.py:17
  178.6 9.3 %fusion = f32[512,768]{1,0:T(8,128)S(1)} fusion(bf16[512,6144]{1,0:T(8,128)(2,1)} %all-gather.4.cloned.1.call-done, bf16[6144,768]{1,0:T(8,128)(2,1)} %all-gather.6.cloned.1.call-done), kind=kOutput, calls=%fused_computation.1 | convolution fusion | flops 4831838208 | bytes 17301504 | tf_op jit(solution)/shard_map/dot_general | solution.py:8
  188.0 73.5 %all-gather.8.cloned.1.call-done = bf16[6144,768]{1,0:T(8,128)(2,1)} async-done(((bf16[384,768]{1,0:T(8,128)(2,1)}), bf16[6144,768]{1,0:T(8,128)(2,1)}) %all-gather.8.cloned.1.call-update) | async-done | bytes 9437200 | tf_op jit(solution)/shard_map/all_gather | solution.py:18
  261.5 10.7 %multiply_multiply_fusion = f32[512,768]{1,0:T(8,128)} fusion(f32[512,768]{1,0:T(8,128)S(1)} %fusion, bf16[512,6144]{1,0:T(8,128)(2,1)} %all-gather.4.cloned.1.call-done, bf16[6144,768]{1,0:T(8,128)(2,1)} %all-gather.8.cloned.1.call-done), kind=kOutput, calls=%fused_computation | convolution fusion | flops 4833804288 | bytes 18874368 | tf_op jit(solution)/shard_map/dot_general | solution.py:8
Async XLA Ops:
  6.5 84.5 %all-gather.4.cloned.1.call-start = ((), (), s32[]{:S(2)}) async-start(), calls=%async_computation | async-start | bytes 6684672 | tf_op jit(solution)/shard_map/all_gather | solution.py:12
  7.3 171.4 %all-gather.6.cloned.1.call-start = ((), (), s32[]{:S(2)}) async-start(), calls=%async_computation.1 | async-start | bytes 10027008 | tf_op jit(solution)/shard_map/all_gather | solution.py:17
  8.0 253.5 %all-gather.8.cloned.1.call-start = ((), (), s32[]{:S(2)}) async-start(), calls=%async_computation.2 | async-start | bytes 10027008 | tf_op jit(solution)/shard_map/all_gather | solution.py:18
Sparse Core Ops, SparseCore 0:
  9.2 81.8 all-gather.3
  93.8 84.7 all-gather.5
  181.4 80.0 all-gather.7
where the time goes:
time: 279 us
  waiting for transfers between devices  246 us (88%)
  matrix products  20.1 us (7%)
  between operations  13.1 us (5%)
    all_gather x1, waiting for transfers between devices, per_device(): lax.all_gather(gate_weight, 'row', axis=0, tiled=True)  87.6 us
    all_gather x1, waiting for transfers between devices, per_device(): gathered = lax.all_gather(tokens, 'col', axis=1, tiled=True)  82.3 us
    all_gather x1, waiting for transfers between devices, per_device(): up_sum = add_single(lax.all_gather(up_weight, 'row', axis=0, tiled=True))  73.5 us
    dot_general x2, matrix products, accumulate(): return jnp.dot(gathered, weight_rows, preferred_element_type=jnp.float32)  20.1 us
  transfers between devices with their start and end apart: 3, of which 3 were waited for; matrix products, arithmetic and copies ran while one was open for 3% of the time, Pallas kernels for 0%

commit v1 on v0

--- a/solution.py
+++ b/solution.py
@@ -14,7 +14,11 @@
     def add_single(weight_rows):
         return accumulate(gathered, weight_rows)
 
-    gate_sum = add_single(lax.all_gather(gate_weight, "row", axis=0, tiled=True))
+    gate_sum = add_single(
+        jnp.concatenate(
+            lax.all_to_all(jnp.stack([gate_weight] * lax.axis_size("row")), "row", 0, 0), axis=0
+        )
+    )
     up_sum = add_single(lax.all_gather(up_weight, "row", axis=0, tiled=True))
     return jax.nn.silu(gate_sum) * up_sum
 

time: 279 us -> 269 us (0.964)
  waiting for transfers between devices: 246 us -> 52.3 us
  blocking collectives: 0 us -> 181 us
    all_to_all x0 -> x1, blocking collectives: none -> 181 us  [per_device(): lax.all_to_all(jnp.stack([gate_weight] * lax.axis_size('row')), 'row', 0, 0)]
    all_gather x1 -> x0, waiting for transfers between devices: 87.6 us -> none  [per_device(): lax.all_gather(gate_weight, 'row', axis=0, tiled=True)]
    all_gather x1, waiting for transfers between devices: 82.3 us -> 0.01 us  [per_device(): gathered = lax.all_gather(tokens, 'col', axis=1, tiled=True)]
    all_gather x1, waiting for transfers between devices: 73.5 us -> 50.9 us  [per_device(): up_sum = add_single(lax.all_gather(up_weight, 'row', axis=0, tiled=True))]
  transfers between devices with their start and end apart: 3 -> 2, of which waited for: 3 -> 1; matrix products, arithmetic and copies ran while one was open for 3% -> 4% of each run, Pallas kernels for 0% -> 0%
where the time goes in v1:
time: 269 us
  blocking collectives  181 us (67%)
  waiting for transfers between devices  52.3 us (19%)
  matrix products  20.1 us (7%)
  between operations  13.4 us (5%)
    all_to_all x1, blocking collectives, per_device(): lax.all_to_all(jnp.stack([gate_weight] * lax.axis_size('row')), 'row', 0, 0)  181 us
    all_gather x1, waiting for transfers between devices, per_device(): up_sum = add_single(lax.all_gather(up_weight, 'row', axis=0, tiled=True))  50.9 us
    dot_general x2, matrix products, accumulate(): return jnp.dot(gathered, weight_rows, preferred_element_type=jnp.float32)  20.1 us
  transfers between devices with their start and end apart: 2, of which 1 were waited for; matrix products, arithmetic and copies ran while one was open for 4% of the time, Pallas kernels for 0%

profile of v1, /device:TPU:1, one launch (start us, length us, event | category | flops | bytes accessed | tf_op | source)
XLA Modules:
  0.0 268.8 jit_solution(14696800534953230165)
XLA Ops:
  6.5 0.0 all-gather.3.cloned.1.call-start
  6.5 0.7 all-gather.3.cloned.1.call-update
  7.3 0.0 all-gather.5.cloned.1.call-start
  7.3 0.7 all-gather.5.cloned.1.call-update
  8.0 2.0 stack.2
  10.0 180.9 %all_to_all.5 = bf16[16,384,768]{2,1,0:T(8,128)(2,1)} all-to-all(bf16[16,384,768]{2,1,0:T(8,128)(2,1)S(1)} %stack.2), channel_id=1, replica_groups=mesh['row'=16,'col'=16] {'row'}, dimensions={0} | all-to-all | bytes 18874368 | tf_op jit(solution)/shard_map/all_to_all | solution.py:19
  190.9 0.0 all-gather.3.cloned.1.call-done
  190.9 9.4 %fusion = f32[512,768]{1,0:T(8,128)S(1)} fusion(bf16[512,6144]{1,0:T(8,128)(2,1)} %all-gather.3.cloned.1.call-done, bf16[6144,768]{1,0:T(8,128)(2,1)} %bitcast.5), kind=kOutput, calls=%fused_computation.1 | convolution fusion | flops 4831838208 | bytes 17301504 | tf_op jit(solution)/shard_map/dot_general | solution.py:8
  200.3 50.9 %all-gather.5.cloned.1.call-done = bf16[6144,768]{1,0:T(8,128)(2,1)} async-done(((bf16[384,768]{1,0:T(8,128)(2,1)}), bf16[6144,768]{1,0:T(8,128)(2,1)}) %all-gather.5.cloned.1.call-update) | async-done | bytes 9437200 | tf_op jit(solution)/shard_map/all_gather | solution.py:22
  251.2 10.7 %multiply_multiply_fusion = f32[512,768]{1,0:T(8,128)} fusion(f32[512,768]{1,0:T(8,128)S(1)} %fusion, bf16[512,6144]{1,0:T(8,128)(2,1)} %all-gather.3.cloned.1.call-done, bf16[6144,768]{1,0:T(8,128)(2,1)} %all-gather.5.cloned.1.call-done), kind=kOutput, calls=%fused_computation | convolution fusion | flops 4833804288 | bytes 18874368 | tf_op jit(solution)/shard_map/dot_general | solution.py:8
Async XLA Ops:
  6.5 184.4 %all-gather.3.cloned.1.call-start = ((), (), s32[]{:S(2)}) async-start(), calls=%async_computation.1 | async-start | bytes 6684672 | tf_op jit(solution)/shard_map/all_gather | solution.py:12
  7.3 243.9 %all-gather.5.cloned.1.call-start = ((), (), s32[]{:S(2)}) async-start(), calls=%async_computation.2 | async-start | bytes 10027008 | tf_op jit(solution)/shard_map/all_gather | solution.py:22
Sparse Core Ops, SparseCore 0:
  9.2 155.6 all-gather.2
  167.5 83.6 all-gather.4
